TPU v7x, 32 devices: a whole 2x2x4 slice. The times are simulated.
32 devices in a mesh: dom: 8 (over z, x), band: 4 (over y, core).
Axes of the slice: x: 2, y: 2, z: 4, core: 2. Of those that a mesh axis runs over, the one named last changes fastest.
Arguments:
- orbitals: float32 [32, 96, 64, 128], P('band', 'dom'), may hold values from -1400 to 1400
- potential: float32 [96, 64, 128], P('dom'), may hold values from 0.1 to 2
Outputs:
- ortho_orbitals: float32 [32, 96, 64, 128], P('band', 'dom')
All inputs are finite; a program needn't handle non-finite values.
Results may differ from a plain program's by a relative error of at most 0.0003.
Values sent between devices are 32-bit elements; how exact they have to be, the bound alone decides.
A program may use at most 64 MiB of HBM per device.

v0:
```python
import functools
import jax
import jax.numpy as jnp
from jax import lax
from jax.experimental import pallas as pl
from jax.experimental.pallas import tpu as pltpu
from jax.sharding import PartitionSpec as P

stencil_weights = [
    -5369.0 / 1800.0,
    12.0 / 7.0,
    -15.0 / 56.0,
    10.0 / 189.0,
    -1.0 / 112.0,
    2.0 / 1925.0,
    -1.0 / 16632.0,
]
center_shift = 9.5
half_width = 7.5
reach = 6
pad = 8
scaled = [-0.5 * w / half_width for w in stencil_weights]
HIGHEST = lax.Precision.HIGHEST
MESH = pl.DeviceIdType.MESH


def divisor(n, options):
    for c in options:
        if n % c == 0:
            return c
    return 1


def packed_rows(total, nz):
    fold = nz // total if total < nz and nz % total == 0 else 1
    return total // fold if total % (8 * fold) == 0 else total


def kernel(
    doms, bands, nb, nx, ny, nz,
    orb, pot, out,
    bz, u, f, own_f, ret_f, potb, cells, obuf, gs, ar1, ar2, inv,
    own_sem, pot_sem, pot_s, pot_r, swap_s, swap_r, h1_s, h1_r, h2_s, h2_r,
    ret_s, ret_r, core_s, core_r, loc_s, y_s, y_r,
    r1_s, r1_r, r2_s, r2_r, out_s, out_r, out_l,
):
    half = nb // 2
    planes = 2 * nx
    total = nb * bands
    group = 2 * bands
    chips = bands // 2
    slab = nx * ny
    part = slab // 2
    share = part // chips
    dom = lax.axis_index("dom")
    band = lax.axis_index("band")
    layer = dom // 2
    layers = doms // 2
    side = dom % 2
    row = band // 2
    core = band % 2
    base = layer * 2
    me = side * bands + band
    partner = {"dom": base + 1 - side, "band": band}
    sibling = {"dom": dom, "band": row * 2 + 1 - core}
    inner, outer = 1 - side, side

    def peer_id(j):
        g = (me + j) % group
        return {"dom": base + g // bands, "band": g % bands}

    def layer_id(j):
        return {"dom": ((layer + j) % layers) * 2 + side, "band": band}

    barrier = pltpu.get_barrier_semaphore()
    for j in range(1, group):
        pl.semaphore_signal(barrier, inc=1, device_id=peer_id(j), device_id_type=MESH)
    for j in range(1, layers):
        pl.semaphore_signal(barrier, inc=1, device_id=layer_id(j), device_id_type=MESH)
    pl.semaphore_wait(barrier, group - 1 + layers - 1)

    def remote(src, dst, s, r, dev):
        return pltpu.make_async_remote_copy(
            src_ref=src, dst_ref=dst, send_sem=s, recv_sem=r, device_id=dev, device_id_type=MESH
        )

    rows = pl.ds(pad, ny)

    def swap(o, p):
        first = (outer if p == 0 else inner) * reach
        return remote(
            orb.at[(1 - side) * half + o, pl.ds(first, reach)],
            u.at[o, pl.ds(reach + side * nx + first, reach), rows],
            swap_s.at[p, o], swap_r.at[p, o], partner,
        )

    pot_share = slab // bands
    pot_rows = pl.ds(pl.multiple_of(band * pot_share, 8), pot_share)
    my_pot = pl.ds(pl.multiple_of(side * slab + band * pot_share, 8), pot_share)
    got_pot = pl.ds(pl.multiple_of((1 - side) * slab + band * pot_share, 8), pot_share)
    swap_pot = remote(pot.at[pot_rows], potb.at[my_pot], pot_s.at[0], pot_r.at[0], partner)

    def pass_pot(j):
        return remote(
            potb.at[got_pot], potb.at[got_pot], pot_s.at[j], pot_r.at[j],
            {"dom": dom, "band": (band + j) % bands},
        )

    def own(o):
        return pltpu.make_async_copy(
            orb.at[side * half + o], u.at[o, pl.ds(reach + side * nx, nx), rows], own_sem.at[o]
        )

    own_pot = pltpu.make_async_copy(
        pot, potb.at[pl.ds(pl.multiple_of(side * slab, 8), slab)], pot_sem
    )

    swap_pot.start()
    for o in range(half):
        for p in range(2):
            swap(o, p).start()
    for o in range(half):
        own(o).start()
    own_pot.start()

    def up(buf, o, s, r):
        return remote(
            buf.at[o, pl.ds(planes, reach), rows], buf.at[o, pl.ds(0, reach), rows],
            s.at[0, o], r.at[0, o], {"dom": dom + 2, "band": band},
        )

    def down(buf, o, s, r):
        return remote(
            buf.at[o, pl.ds(reach, reach), rows], buf.at[o, pl.ds(planes + reach, reach), rows],
            s.at[1, o], r.at[1, o], {"dom": dom - 2, "band": band},
        )

    has_up = layer < layers - 1
    has_down = layer > 0

    def send_face(buf, o, s, r, which):
        @pl.when(jnp.logical_and(has_up, side == which))
        def _():
            up(buf, o, s, r).start()

        @pl.when(jnp.logical_and(has_down, side == 1 - which))
        def _():
            down(buf, o, s, r).start()

    def wait_halos(buf, o, s, r):
        @pl.when(has_down)
        def _():
            up(buf, o, s, r).wait_recv()

        @pl.when(has_up)
        def _():
            down(buf, o, s, r).wait_recv()

    distance = jnp.abs(
        lax.broadcasted_iota(jnp.int32, (nz, nz), 0) - lax.broadcasted_iota(jnp.int32, (nz, nz), 1)
    )
    banded = jnp.zeros((nz, nz), jnp.float32)
    for k in range(1, reach + 1):
        banded = jnp.where(distance == k, jnp.float32(scaled[k]), banded)
    bz[...] = banded
    edge = jnp.zeros((planes + 2 * reach, pad, nz), jnp.float32)
    for buf in (u, f):
        for o in range(half):
            buf[o, :, pl.ds(0, pad), :] = edge
            buf[o, :, pl.ds(pad + ny, pad), :] = edge
    empty = jnp.zeros((reach, ny, nz), jnp.float32)
    for buf in (u, f):
        for o in range(half):
            @pl.when(jnp.logical_not(has_down))
            def _():
                buf[o, pl.ds(0, reach), rows, :] = empty

            @pl.when(jnp.logical_not(has_up))
            def _():
                buf[o, pl.ds(planes + reach, reach), rows, :] = empty

    for q in range(1, chips):
        @pl.when(row < q)
        def _():
            for i in range(q * 2 * nb, (q + 1) * 2 * nb):
                for p in range(1, chips):
                    first = pl.multiple_of(i * part + ((row + p) % chips) * share, 8)
                    cells[pl.ds(first, share), :] = jnp.zeros((share, nz), jnp.float32)

    def apply(buf, o, first, count, emit):
        step = divisor(count, (4, 3, 2))

        def body(t, carry):
            x0 = first + t * step
            centre = [buf[o, reach + x0 + i, pl.ds(pad, ny), :] for i in range(step)]
            along_z = jnp.dot(
                jnp.concatenate(centre, axis=0), bz[...], precision=HIGHEST,
                preferred_element_type=jnp.float32,
            )
            for i in range(step):
                x = reach + x0 + i
                weight = potb[pl.ds(pl.multiple_of((x0 + i) * ny, 8), ny), :] * (1.0 / half_width) + (
                    3.0 * scaled[0] - center_shift / half_width
                )
                acc = along_z[i * ny:(i + 1) * ny] + weight * centre[i]
                for k in range(1, reach + 1):
                    near = buf[o, x + k, pl.ds(pad, ny), :] + buf[o, x - k, pl.ds(pad, ny), :]
                    near = near + (
                        buf[o, x, pl.ds(pad + k, ny), :] + buf[o, x, pl.ds(pad - k, ny), :]
                    )
                    acc = acc + scaled[k] * near
                emit(x0 + i, acc)
            return carry

        lax.fori_loop(0, count // step, body, 0)

    def first_term(o, first, count):
        def emit(x, acc):
            f[o, reach + x, pl.ds(pad, ny), :] = acc

        apply(u, o, first, count, emit)

    def second_term(o, slab_side, which, dst, k):
        def emit(x, acc):
            start = pl.multiple_of((x - slab_side * nx) * ny, 8)
            dst[k, pl.ds(start, ny), :] = 2.0 * acc - u[o, reach + x, pl.ds(pad, ny), :]

        apply(f, o, slab_side * nx + which * reach, reach, emit)

    def y_copy(j, k, h, p):
        to = (row + j) % chips
        at = ((to + p) % chips) * share
        return remote(
            own_f.at[k, pl.ds(pl.multiple_of(h * part + at, 8), share)],
            cells.at[pl.ds(pl.multiple_of((band * nb + k) * part + at, 8), share)],
            y_s.at[j - 1, h, k, p], y_r.at[j - 1, core, k, p],
            {"dom": dom, "band": to * 2 + h},
        )

    def y_got(j, c, k, p):
        to = row
        at = ((to + p) % chips) * share
        from_band = ((row - j + chips) % chips) * 2 + c
        return remote(
            own_f.at[k, pl.ds(pl.multiple_of(at, 8), share)],
            cells.at[pl.ds(pl.multiple_of((from_band * nb + k) * part + at, 8), share)],
            y_s.at[j - 1, 0, k, p], y_r.at[j - 1, c, k, p],
            {"dom": dom, "band": ((row + j) % chips) * 2},
        )

    def core_copy(k):
        return remote(
            own_f.at[k, pl.ds(pl.multiple_of((1 - core) * part, 8), part)],
            cells.at[pl.ds(pl.multiple_of((band * nb + k) * part, 8), part)],
            core_s.at[k], core_r.at[k], sibling,
        )

    def local_copy(k):
        return pltpu.make_async_copy(
            own_f.at[k, pl.ds(pl.multiple_of(core * part, 8), part)],
            cells.at[pl.ds(pl.multiple_of((band * nb + k) * part, 8), part)],
            loc_s.at[k],
        )

    def spread(k, h):
        for j in range(1, chips):
            y_copy(j, k, h, 0).start()

        @pl.when(h != core)
        def _():
            core_copy(k).start()

        @pl.when(h == core)
        def _():
            local_copy(k).start()

    def spread_rest(k, h):
        for j in range(1, chips):
            @pl.when((row + j) % chips > row)
            def _():
                for p in range(1, chips):
                    y_copy(j, k, h, p).start()

    def back(o, h):
        at = pl.ds(pl.multiple_of(h * part, 8), part)
        return remote(
            ret_f.at[o, at], own_f.at[side * half + o, at], ret_s.at[h, o], ret_r.at[h, o], partner
        )

    def came(o, h):
        at = pl.ds(pl.multiple_of(h * part, 8), part)
        return remote(
            ret_f.at[o, at], own_f.at[(1 - side) * half + o, at], ret_s.at[h, o], ret_r.at[h, o], partner
        )

    def finish(o, which):
        k = side * half + o
        second_term(o, side, which, own_f, k)
        spread(k, which)
        spread_rest(k, which)
        second_term(o, 1 - side, 1 - which, ret_f, o)
        back(o, 1 - which).start()

    def returned(o, which):
        came(o, which).wait_recv()
        spread((1 - side) * half + o, which)

    def late(o, which):
        spread_rest((1 - side) * half + o, which)

    swap_pot.wait_recv()
    for j in range(1, bands):
        pass_pot(j).start()
    for o in range(min(2, half)):
        own(o).wait()
        send_face(u, o, h1_s, h1_r, 1)
    own_pot.wait()

    for o in range(half):
        swap(o, 0).wait_recv()
        send_face(u, o, h1_s, h1_r, 0)
        if o == 0:
            for j in range(1, bands):
                pass_pot(j).wait_recv()
        swap(o, 1).wait_recv()
        first_term(o, reach, planes - 2 * reach)
        if o > 0:
            wait_halos(f, o - 1, h2_s, h2_r)
            finish(o - 1, outer)
        wait_halos(u, o, h1_s, h1_r)
        first_term(o, 0, reach)
        first_term(o, planes - reach, reach)
        send_face(f, o, h2_s, h2_r, 1)
        send_face(f, o, h2_s, h2_r, 0)
        if o + 2 < half:
            own(o + 2).wait()
            send_face(u, o + 2, h1_s, h1_r, 1)
        finish(o, inner)
    returned(0, inner)
    wait_halos(f, half - 1, h2_s, h2_r)
    finish(half - 1, outer)
    returned(0, outer)
    for o in range(1, half):
        returned(o, inner)
        late(o - 1, inner) if o < half - 1 else None
        returned(o, outer)
        late(o - 1, outer) if o < half - 1 else None
    for o in range(max(half - 2, 0), half):
        late(o, inner)
        late(o, outer)

    for k in range(nb):
        local_copy(k).wait()
        core_copy(k).wait_recv()
        for j in range(1, chips):
            for c in range(2):
                y_got(j, c, k, 0).wait_recv()

    packed = packed_rows(total, nz)
    chunk = divisor(share, (16, 8))

    def gather(first):
        return jnp.concatenate(
            [cells[pl.ds(first + i, total, stride=part), :] for i in range(chunk)], axis=1
        )

    mine = row * share

    def gram_body(t, acc):
        x = gather(mine + t * chunk)
        return acc + lax.dot_general(
            x, x, (((1,), (1,)), ((), ())), precision=HIGHEST, preferred_element_type=jnp.float32
        )

    gram = lax.fori_loop(0, share // chunk, gram_body, jnp.zeros((total, total), jnp.float32))
    gram = jnp.concatenate(
        [gram[i * packed:(i + 1) * packed] for i in range(total // packed)], axis=1
    )
    gs[0] = gram
    ar1[me] = gram

    def reduce_1(j):
        return remote(gs.at[0], ar1.at[me], r1_s.at[j - 1], r1_r.at[j - 1], peer_id(j))

    def reduce_2(j):
        return remote(gs.at[1], ar2.at[layer], r2_s.at[j - 1], r2_r.at[j - 1], layer_id(j))

    for j in range(1, group):
        reduce_1(j).start()
    for j in range(1, group):
        reduce_1(j).wait_recv()
    total_1 = ar1[0]
    for j in range(1, group):
        total_1 = total_1 + ar1[j]
    gs[1] = total_1
    ar2[layer] = total_1
    for j in range(1, layers):
        reduce_2(j).start()
    for j in range(1, layers):
        reduce_2(j).wait_recv()
    work = ar2[0]
    for j in range(1, layers):
        work = work + ar2[j]

    work = jnp.concatenate(
        [work[:, i * total:(i + 1) * total] for i in range(total // packed)], axis=0
    )
    work = jnp.concatenate([work, jnp.zeros((total, total), jnp.float32)], axis=1)
    lane = lax.broadcasted_iota(jnp.int32, work.shape, 1)
    line = lax.broadcasted_iota(jnp.int32, work.shape, 0)
    work = work / jnp.float32(slab * doms * nz)
    work = jnp.where(lane == line + total, jnp.float32(1.0), work)
    for k in range(total):
        root = jnp.sqrt(work[k:k + 1, k:k + 1])
        scale = 1.0 / root
        pivot = work[k:k + 1, :] * scale
        column = work[:, k:k + 1] * scale
        work = jnp.where(line > k, work - column * pivot, jnp.where(line == k, pivot, work))
    pair = 2 * nb
    for q in range(chips):
        inv[q] = work[q * pair:(q + 1) * pair, total:2 * total]

    pieces = divisor(share // chunk, (4, 3, 2))
    piece = share // pieces
    obuf3 = obuf.reshape(pair, part, nz)

    def give(p, s):
        at = pl.multiple_of(((row + p) % chips) * share + s * piece, 8)
        return remote(
            obuf3.at[pl.ds((1 - core) * nb, nb), pl.ds(at, piece)],
            out.at[:, pl.ds(core * part + at, piece)],
            out_s.at[p, s], out_r.at[p, s], sibling,
        )

    def keep(p, s):
        at = pl.multiple_of(((row + p) % chips) * share + s * piece, 8)
        return pltpu.make_async_copy(
            obuf3.at[pl.ds(core * nb, nb), pl.ds(at, piece)],
            out.at[:, pl.ds(core * part + at, piece)], out_l.at[p, s],
        )

    for p in range(chips):
        if p > 0:
            for j in range(1, chips):
                @pl.when((row - j + chips) % chips < row)
                def _():
                    for k in range(nb):
                        for c in range(2):
                            y_got(j, c, k, p).wait_recv()
        at_part = ((row + p) % chips) * share

        def piece_body(s, carry):
            def ortho_body(t, carry):
                first = at_part + s * piece + t * chunk
                y = jnp.dot(inv[row], gather(first), precision=HIGHEST, preferred_element_type=jnp.float32)
                for i in range(chunk):
                    obuf[pl.ds(first + i, pair, stride=part), :] = y[:, i * nz:(i + 1) * nz]
                return carry

            lax.fori_loop(0, piece // chunk, ortho_body, 0)
            give(p, s).start()
            keep(p, s).start()
            return carry

        lax.fori_loop(0, pieces, piece_body, 0)

    swap_pot.wait_send()
    for j in range(1, bands):
        pass_pot(j).wait_send()
    for o in range(half):
        for p in range(2):
            swap(o, p).wait_send()
            back(o, p).wait_send()

        @pl.when(has_up)
        def _():
            up(u, o, h1_s, h1_r).wait_send()
            up(f, o, h2_s, h2_r).wait_send()

        @pl.when(has_down)
        def _():
            down(u, o, h1_s, h1_r).wait_send()
            down(f, o, h2_s, h2_r).wait_send()

    for k in range(nb):
        core_copy(k).wait_send()
        for j in range(1, chips):
            for h in range(2):
                y_copy(j, k, h, 0).wait_send()

            @pl.when((row + j) % chips > row)
            def _():
                for h in range(2):
                    for p in range(1, chips):
                        y_copy(j, k, h, p).wait_send()
    for j in range(1, group):
        reduce_1(j).wait_send()
    for j in range(1, layers):
        reduce_2(j).wait_send()
    for p in range(chips):
        for s in range(pieces):
            keep(p, s).wait()
            give(p, s).wait()


def deliver(held, out, sem):
    copy = pltpu.make_async_copy(held, out, sem)
    copy.start()
    copy.wait()


def shards(doms, bands, orbitals, potential):
    nb, nx, ny, nz = orbitals.shape
    half = nb // 2
    total = nb * bands
    group = 2 * bands
    layers = doms // 2
    chips = bands // 2
    slab = nx * ny
    part = slab // 2
    share = part // chips
    pair = 2 * nb
    dma = pltpu.SemaphoreType.DMA
    f32 = jnp.float32
    packed = packed_rows(total, nz)
    wide = total * total // packed
    pieces = divisor(share // divisor(share, (16, 8)), (4, 3, 2))
    others = max(chips - 1, 1)
    out = pl.pallas_call(
        functools.partial(kernel, doms, bands, nb, nx, ny, nz),
        out_shape=pltpu.VMEM((nb, slab, nz), f32),
        in_specs=[
            pl.BlockSpec(memory_space=pl.ANY),
            pl.BlockSpec(memory_space=pl.ANY),
        ],
        out_specs=pl.BlockSpec(memory_space=pltpu.VMEM),
        scratch_shapes=[
            pltpu.VMEM((nz, nz), f32),
            pltpu.VMEM((half, 2 * nx + 2 * reach, ny + 2 * pad, nz), f32),
            pltpu.VMEM((half, 2 * nx + 2 * reach, ny + 2 * pad, nz), f32),
            pltpu.VMEM((nb, slab, nz), f32),
            pltpu.VMEM((half, slab, nz), f32),
            pltpu.VMEM((2 * slab, nz), f32),
            pltpu.VMEM((total * part, nz), f32),
            pltpu.VMEM((pair * part, nz), f32),
            pltpu.VMEM((2, packed, wide), f32),
            pltpu.VMEM((group, packed, wide), f32),
            pltpu.VMEM((layers, packed, wide), f32),
            pltpu.VMEM((chips, pair, total), f32),
            dma((half,)),
            dma,
            dma((bands,)),
            dma((bands,)),
            dma((2, half)),
            dma((2, half)),
            dma((2, half)),
            dma((2, half)),
            dma((2, half)),
            dma((2, half)),
            dma((2, half)),
            dma((2, half)),
            dma((nb,)),
            dma((nb,)),
            dma((nb,)),
            dma((others, 2, nb, chips)),
            dma((others, 2, nb, chips)),
            dma((group - 1,)),
            dma((group - 1,)),
            dma((max(layers - 1, 1),)),
            dma((max(layers - 1, 1),)),
            dma((chips, pieces)),
            dma((chips, pieces)),
            dma((chips, pieces)),
        ],
        compiler_params=pltpu.CompilerParams(
            collective_id=0, has_side_effects=True, vmem_limit_bytes=60 * 1024 * 1024
        ),
    )(orbitals, potential.reshape(slab, nz))
    out = pl.pallas_call(
        deliver,
        out_shape=jax.ShapeDtypeStruct((nb, slab, nz), f32),
        in_specs=[pl.BlockSpec(memory_space=pl.ANY)],
        out_specs=pl.BlockSpec(memory_space=pl.ANY),
        scratch_shapes=[dma],
        compiler_params=pltpu.CompilerParams(vmem_limit_bytes=16 * 1024 * 1024),
    )(pltpu.with_memory_space_constraint(out, pltpu.VMEM))
    return out.reshape(orbitals.shape)


def solution(mesh):
    in_specs = (P("band", "dom", None, None), P("dom", None, None))
    out_specs = P("band", "dom", None, None)
    body = functools.partial(shards, mesh.shape["dom"], mesh.shape["band"])
    return jax.shard_map(body, mesh=mesh, in_specs=in_specs, out_specs=out_specs, check_vma=False)
```

profile of v0, /device:TPU:0, one launch (start us, length us, event | category | flops | bytes accessed | tf_op | source)
XLA Modules:
  0.0 116.7 jit_solution(7835665275671622555)
XLA Ops:
  0.0 115.1 %shard_map.28.held = f32[8,768,128]{2,1,0:T(8,128)S(1)} custom-call(f32[8,12,64,128]{3,2,1,0:T(8,128)} %orb.1, f32[768,128]{1,0:T(8,128)} %bitcast.2), custom_call_target="tpu_custom_call" | custom-call | tf_op jit(solution)/shard_map/pallas_call | solution.py:529
  115.1 1.7 %shard_map.29 = f32[8,768,128]{2,1,0:T(8,128)} custom-call(f32[8,768,128]{2,1,0:T(8,128)S(1)} %shard_map.28.held), custom_call_target="tpu_custom_call" | custom-call | tf_op jit(solution)/shard_map/pallas_call | solution.py:579
where the time goes:
time: 117 us
  Pallas kernels  117 us (100%)
    pallas_call x1, Pallas kernels, shards(): pl.pallas_call(functools.partial(kernel, doms, bands, nb, nx, ny, nz), ou...  115 us

commit v1 on v0

--- a/solution.py
+++ b/solution.py
@@ -21,6 +21,7 @@
 pad = 8
 scaled = [-0.5 * w / half_width for w in stencil_weights]
 HIGHEST = lax.Precision.HIGHEST
+HIGH = lax.Precision.HIGH
 MESH = pl.DeviceIdType.MESH
 
 
@@ -182,10 +183,11 @@
     for q in range(1, chips):
         @pl.when(row < q)
         def _():
-            for i in range(q * 2 * nb, (q + 1) * 2 * nb):
-                for p in range(1, chips):
-                    first = pl.multiple_of(i * part + ((row + p) % chips) * share, 8)
-                    cells[pl.ds(first, share), :] = jnp.zeros((share, nz), jnp.float32)
+            for p in range(1, chips):
+                at = ((row + p) % chips) * share
+                cells[pl.ds(at, share), pl.ds(q * 2 * nb, 2 * nb), :] = jnp.zeros(
+                    (share, 2 * nb, nz), jnp.float32
+                )
 
     def apply(buf, o, first, count, emit):
         step = divisor(count, (4, 3, 2))
@@ -232,7 +234,7 @@
         at = ((to + p) % chips) * share
         return remote(
             own_f.at[k, pl.ds(pl.multiple_of(h * part + at, 8), share)],
-            cells.at[pl.ds(pl.multiple_of((band * nb + k) * part + at, 8), share)],
+            cells.at[pl.ds(at, share), band * nb + k],
             y_s.at[j - 1, h, k, p], y_r.at[j - 1, core, k, p],
             {"dom": dom, "band": to * 2 + h},
         )
@@ -243,7 +245,7 @@
         from_band = ((row - j + chips) % chips) * 2 + c
         return remote(
             own_f.at[k, pl.ds(pl.multiple_of(at, 8), share)],
-            cells.at[pl.ds(pl.multiple_of((from_band * nb + k) * part + at, 8), share)],
+            cells.at[pl.ds(at, share), from_band * nb + k],
             y_s.at[j - 1, 0, k, p], y_r.at[j - 1, c, k, p],
             {"dom": dom, "band": ((row + j) % chips) * 2},
         )
@@ -251,14 +253,14 @@
     def core_copy(k):
         return remote(
             own_f.at[k, pl.ds(pl.multiple_of((1 - core) * part, 8), part)],
-            cells.at[pl.ds(pl.multiple_of((band * nb + k) * part, 8), part)],
+            cells.at[:, band * nb + k],
             core_s.at[k], core_r.at[k], sibling,
         )
 
     def local_copy(k):
         return pltpu.make_async_copy(
             own_f.at[k, pl.ds(pl.multiple_of(core * part, 8), part)],
-            cells.at[pl.ds(pl.multiple_of((band * nb + k) * part, 8), part)],
+            cells.at[:, band * nb + k],
             loc_s.at[k],
         )
 
@@ -336,18 +338,19 @@
             own(o + 2).wait()
             send_face(u, o + 2, h1_s, h1_r, 1)
         finish(o, inner)
-    returned(0, inner)
+    units = [(o, w) for o in range(half) for w in (inner, outer)]
+    ahead = 4
+    returned(*units[0])
     wait_halos(f, half - 1, h2_s, h2_r)
     finish(half - 1, outer)
-    returned(0, outer)
-    for o in range(1, half):
-        returned(o, inner)
-        late(o - 1, inner) if o < half - 1 else None
-        returned(o, outer)
-        late(o - 1, outer) if o < half - 1 else None
-    for o in range(max(half - 2, 0), half):
-        late(o, inner)
-        late(o, outer)
+    for i in range(1, len(units)):
+        returned(*units[i])
+        if i >= ahead:
+            late(*units[i - ahead])
+    held = max(len(units) - ahead, 0)
+    for i in range(held, min(held + 1, len(units))):
+        late(*units[i])
+    held = min(held + 1, len(units))
 
     for k in range(nb):
         local_copy(k).wait()
@@ -357,12 +360,11 @@
                 y_got(j, c, k, 0).wait_recv()
 
     packed = packed_rows(total, nz)
-    chunk = divisor(share, (16, 8))
+    chunk = divisor(share, (64, 32, 16, 8))
 
     def gather(first):
-        return jnp.concatenate(
-            [cells[pl.ds(first + i, total, stride=part), :] for i in range(chunk)], axis=1
-        )
+        x = cells[pl.ds(first, chunk)]
+        return jnp.concatenate([x[i] for i in range(chunk)], axis=1)
 
     mine = row * share
 
@@ -387,6 +389,8 @@
 
     for j in range(1, group):
         reduce_1(j).start()
+    for i in range(held, len(units)):
+        late(*units[i])
     for j in range(1, group):
         reduce_1(j).wait_recv()
     total_1 = ar1[0]
@@ -422,21 +426,20 @@
 
     pieces = divisor(share // chunk, (4, 3, 2))
     piece = share // pieces
-    obuf3 = obuf.reshape(pair, part, nz)
-
-    def give(p, s):
+
+    def give(p, s, k):
         at = pl.multiple_of(((row + p) % chips) * share + s * piece, 8)
         return remote(
-            obuf3.at[pl.ds((1 - core) * nb, nb), pl.ds(at, piece)],
-            out.at[:, pl.ds(core * part + at, piece)],
-            out_s.at[p, s], out_r.at[p, s], sibling,
-        )
-
-    def keep(p, s):
+            obuf.at[pl.ds(at, piece), 1 - core, k],
+            out.at[k, pl.ds(core * part + at, piece)],
+            out_s.at[p, s, k], out_r.at[p, s, k], sibling,
+        )
+
+    def keep(p, s, k):
         at = pl.multiple_of(((row + p) % chips) * share + s * piece, 8)
         return pltpu.make_async_copy(
-            obuf3.at[pl.ds(core * nb, nb), pl.ds(at, piece)],
-            out.at[:, pl.ds(core * part + at, piece)], out_l.at[p, s],
+            obuf.at[pl.ds(at, piece), core, k],
+            out.at[k, pl.ds(core * part + at, piece)], out_l.at[p, s, k],
         )
 
     for p in range(chips):
@@ -452,14 +455,16 @@
         def piece_body(s, carry):
             def ortho_body(t, carry):
                 first = at_part + s * piece + t * chunk
-                y = jnp.dot(inv[row], gather(first), precision=HIGHEST, preferred_element_type=jnp.float32)
+                y = jnp.dot(inv[row], gather(first), precision=HIGH, preferred_element_type=jnp.float32)
                 for i in range(chunk):
-                    obuf[pl.ds(first + i, pair, stride=part), :] = y[:, i * nz:(i + 1) * nz]
+                    for c in range(2):
+                        obuf[first + i, c] = y[c * nb:(c + 1) * nb, i * nz:(i + 1) * nz]
                 return carry
 
             lax.fori_loop(0, piece // chunk, ortho_body, 0)
-            give(p, s).start()
-            keep(p, s).start()
+            for k in range(nb):
+                give(p, s, k).start()
+                keep(p, s, k).start()
             return carry
 
         lax.fori_loop(0, pieces, piece_body, 0)
@@ -499,8 +504,9 @@
         reduce_2(j).wait_send()
     for p in range(chips):
         for s in range(pieces):
-            keep(p, s).wait()
-            give(p, s).wait()
+            for k in range(nb):
+                keep(p, s, k).wait()
+                give(p, s, k).wait()
 
 
 def deliver(held, out, sem):
@@ -524,7 +530,7 @@
     f32 = jnp.float32
     packed = packed_rows(total, nz)
     wide = total * total // packed
-    pieces = divisor(share // divisor(share, (16, 8)), (4, 3, 2))
+    pieces = divisor(share // divisor(share, (64, 32, 16, 8)), (4, 3, 2))
     others = max(chips - 1, 1)
     out = pl.pallas_call(
         functools.partial(kernel, doms, bands, nb, nx, ny, nz),
@@ -541,8 +547,8 @@
             pltpu.VMEM((nb, slab, nz), f32),
             pltpu.VMEM((half, slab, nz), f32),
             pltpu.VMEM((2 * slab, nz), f32),
-            pltpu.VMEM((total * part, nz), f32),
-            pltpu.VMEM((pair * part, nz), f32),
+            pltpu.VMEM((part, total, nz), f32),
+            pltpu.VMEM((part, 2, nb, nz), f32),
             pltpu.VMEM((2, packed, wide), f32),
             pltpu.VMEM((group, packed, wide), f32),
             pltpu.VMEM((layers, packed, wide), f32),
@@ -568,9 +574,9 @@
             dma((group - 1,)),
             dma((max(layers - 1, 1),)),
             dma((max(layers - 1, 1),)),
-            dma((chips, pieces)),
-            dma((chips, pieces)),
-            dma((chips, pieces)),
+            dma((chips, pieces, nb)),
+            dma((chips, pieces, nb)),
+            dma((chips, pieces, nb)),
         ],
         compiler_params=pltpu.CompilerParams(
             collective_id=0, has_side_effects=True, vmem_limit_bytes=60 * 1024 * 1024

time: 117 us -> 108 us (0.923)
  Pallas kernels: 117 us -> 108 us
    pallas_call x1, Pallas kernels: 115 us -> 106 us  [shards(): pl.pallas_call(functools.partial(kernel, doms, bands, nb, nx, ny, nz), ou...]
where the time goes in v1:
time: 108 us
  Pallas kernels  108 us (100%)
    pallas_call x1, Pallas kernels, shards(): pl.pallas_call(functools.partial(kernel, doms, bands, nb, nx, ny, nz), ou...  106 us

profile of v1, /device:TPU:0, one launch (start us, length us, event | category | flops | bytes accessed | tf_op | source)
XLA Modules:
  0.0 108.0 jit_solution(10372693097461665862)
XLA Ops:
  0.0 106.1 %shard_map.28.held = f32[8,768,128]{2,1,0:T(8,128)S(1)} custom-call(f32[8,12,64,128]{3,2,1,0:T(8,128)} %orb.1, f32[768,128]{1,0:T(8,128)} %bitcast.2), custom_call_target="tpu_custom_call" | custom-call | tf_op jit(solution)/shard_map/pallas_call | solution.py:535
  106.1 1.7 %shard_map.29 = f32[8,768,128]{2,1,0:T(8,128)} custom-call(f32[8,768,128]{2,1,0:T(8,128)S(1)} %shard_map.28.held), custom_call_target="tpu_custom_call" | custom-call | tf_op jit(solution)/shard_map/pallas_call | solution.py:585

commit v2 on v1

--- a/solution.py
+++ b/solution.py
@@ -267,7 +267,9 @@
     def spread(k, h):
         for j in range(1, chips):
             y_copy(j, k, h, 0).start()
-
+        spread_chip(k, h)
+
+    def spread_chip(k, h):
         @pl.when(h != core)
         def _():
             core_copy(k).start()
@@ -283,16 +285,20 @@
                 for p in range(1, chips):
                     y_copy(j, k, h, p).start()
 
-    def back(o, h):
-        at = pl.ds(pl.multiple_of(h * part, 8), part)
-        return remote(
-            ret_f.at[o, at], own_f.at[side * half + o, at], ret_s.at[h, o], ret_r.at[h, o], partner
-        )
-
-    def came(o, h):
-        at = pl.ds(pl.multiple_of(h * part, 8), part)
-        return remote(
-            ret_f.at[o, at], own_f.at[(1 - side) * half + o, at], ret_s.at[h, o], ret_r.at[h, o], partner
+    def piece_of(h, q):
+        return pl.ds(pl.multiple_of(h * part + ((row + q) % chips) * share, 8), share)
+
+    def back(o, h, q):
+        at = piece_of(h, q)
+        return remote(
+            ret_f.at[o, at], own_f.at[side * half + o, at], ret_s.at[h, o, q], ret_r.at[h, o, q], partner
+        )
+
+    def came(o, h, q):
+        at = piece_of(h, q)
+        return remote(
+            ret_f.at[o, at], own_f.at[(1 - side) * half + o, at], ret_s.at[h, o, q], ret_r.at[h, o, q],
+            partner,
         )
 
     def finish(o, which):
@@ -301,11 +307,16 @@
         spread(k, which)
         spread_rest(k, which)
         second_term(o, 1 - side, 1 - which, ret_f, o)
-        back(o, 1 - which).start()
+        for q in range(1, chips + 1):
+            back(o, 1 - which, q % chips).start()
 
     def returned(o, which):
-        came(o, which).wait_recv()
-        spread((1 - side) * half + o, which)
+        k = (1 - side) * half + o
+        for q in range(1, chips):
+            came(o, which, q).wait_recv()
+            y_copy(q, k, which, 0).start()
+        came(o, which, 0).wait_recv()
+        spread_chip(k, which)
 
     def late(o, which):
         spread_rest((1 - side) * half + o, which)
@@ -339,7 +350,7 @@
             send_face(u, o + 2, h1_s, h1_r, 1)
         finish(o, inner)
     units = [(o, w) for o in range(half) for w in (inner, outer)]
-    ahead = 4
+    ahead = 6
     returned(*units[0])
     wait_halos(f, half - 1, h2_s, h2_r)
     finish(half - 1, outer)
@@ -348,9 +359,6 @@
         if i >= ahead:
             late(*units[i - ahead])
     held = max(len(units) - ahead, 0)
-    for i in range(held, min(held + 1, len(units))):
-        late(*units[i])
-    held = min(held + 1, len(units))
 
     for k in range(nb):
         local_copy(k).wait()
@@ -371,7 +379,7 @@
     def gram_body(t, acc):
         x = gather(mine + t * chunk)
         return acc + lax.dot_general(
-            x, x, (((1,), (1,)), ((), ())), precision=HIGHEST, preferred_element_type=jnp.float32
+            x, x, (((1,), (1,)), ((), ())), precision=HIGH, preferred_element_type=jnp.float32
         )
 
     gram = lax.fori_loop(0, share // chunk, gram_body, jnp.zeros((total, total), jnp.float32))
@@ -424,7 +432,7 @@
     for q in range(chips):
         inv[q] = work[q * pair:(q + 1) * pair, total:2 * total]
 
-    pieces = divisor(share // chunk, (4, 3, 2))
+    pieces = 1
     piece = share // pieces
 
     def give(p, s, k):
@@ -475,7 +483,8 @@
     for o in range(half):
         for p in range(2):
             swap(o, p).wait_send()
-            back(o, p).wait_send()
+            for q in range(chips):
+                back(o, p, q).wait_send()
 
         @pl.when(has_up)
         def _():
@@ -530,7 +539,7 @@
     f32 = jnp.float32
     packed = packed_rows(total, nz)
     wide = total * total // packed
-    pieces = divisor(share // divisor(share, (64, 32, 16, 8)), (4, 3, 2))
+    pieces = 1
     others = max(chips - 1, 1)
     out = pl.pallas_call(
         functools.partial(kernel, doms, bands, nb, nx, ny, nz),
@@ -563,8 +572,8 @@
             dma((2, half)),
             dma((2, half)),
             dma((2, half)),
-            dma((2, half)),
-            dma((2, half)),
+            dma((2, half, chips)),
+            dma((2, half, chips)),
             dma((nb,)),
             dma((nb,)),
             dma((nb,)),

time: 108 us -> 101 us (0.935)
  Pallas kernels: 108 us -> 100 us
    pallas_call x1, Pallas kernels: 106 us -> 98.7 us  [shards(): pl.pallas_call(functools.partial(kernel, doms, bands, nb, nx, ny, nz), ou...]
where the time goes in v2:
time: 101 us
  Pallas kernels  100 us (99%)
    pallas_call x1, Pallas kernels, shards(): pl.pallas_call(functools.partial(kernel, doms, bands, nb, nx, ny, nz), ou...  98.7 us

profile of v2, /device:TPU:0, one launch (start us, length us, event | category | flops | bytes accessed | tf_op | source)
XLA Modules:
  0.0 100.5 jit_solution(13397218020496142957)
XLA Ops:
  0.0 98.7 %shard_map.28.held = f32[8,768,128]{2,1,0:T(8,128)S(1)} custom-call(f32[8,12,64,128]{3,2,1,0:T(8,128)} %orb.1, f32[768,128]{1,0:T(8,128)} %bitcast.2), custom_call_target="tpu_custom_call" | custom-call | tf_op jit(solution)/shard_map/pallas_call | solution.py:544
  98.7 1.7 %shard_map.29 = f32[8,768,128]{2,1,0:T(8,128)} custom-call(f32[8,768,128]{2,1,0:T(8,128)S(1)} %shard_map.28.held), custom_call_target="tpu_custom_call" | custom-call | tf_op jit(solution)/shard_map/pallas_call | solution.py:594

commit v3 on v2

--- a/solution.py
+++ b/solution.py
@@ -368,7 +368,7 @@
                 y_got(j, c, k, 0).wait_recv()
 
     packed = packed_rows(total, nz)
-    chunk = divisor(share, (64, 32, 16, 8))
+    chunk = divisor(share, (96, 64, 32, 16, 8))
 
     def gather(first):
         x = cells[pl.ds(first, chunk)]
@@ -399,6 +399,30 @@
         reduce_1(j).start()
     for i in range(held, len(units)):
         late(*units[i])
+    swap_pot.wait_send()
+    for j in range(1, bands):
+        pass_pot(j).wait_send()
+    for o in range(half):
+        for p in range(2):
+            swap(o, p).wait_send()
+            for q in range(chips):
+                back(o, p, q).wait_send()
+
+        @pl.when(has_up)
+        def _():
+            up(u, o, h1_s, h1_r).wait_send()
+            up(f, o, h2_s, h2_r).wait_send()
+
+        @pl.when(has_down)
+        def _():
+            down(u, o, h1_s, h1_r).wait_send()
+            down(f, o, h2_s, h2_r).wait_send()
+
+    for k in range(nb):
+        core_copy(k).wait_send()
+        for j in range(1, chips):
+            for h in range(2):
+                y_copy(j, k, h, 0).wait_send()
     for j in range(1, group):
         reduce_1(j).wait_recv()
     total_1 = ar1[0]
@@ -477,31 +501,8 @@
 
         lax.fori_loop(0, pieces, piece_body, 0)
 
-    swap_pot.wait_send()
-    for j in range(1, bands):
-        pass_pot(j).wait_send()
-    for o in range(half):
-        for p in range(2):
-            swap(o, p).wait_send()
-            for q in range(chips):
-                back(o, p, q).wait_send()
-
-        @pl.when(has_up)
-        def _():
-            up(u, o, h1_s, h1_r).wait_send()
-            up(f, o, h2_s, h2_r).wait_send()
-
-        @pl.when(has_down)
-        def _():
-            down(u, o, h1_s, h1_r).wait_send()
-            down(f, o, h2_s, h2_r).wait_send()
-
     for k in range(nb):
-        core_copy(k).wait_send()
         for j in range(1, chips):
-            for h in range(2):
-                y_copy(j, k, h, 0).wait_send()
-
             @pl.when((row + j) % chips > row)
             def _():
                 for h in range(2):

time: 101 us -> 100 us (0.990)
  no operation moved by 1% of the time
where the time goes in v3:
time: 100 us
  Pallas kernels  99.9 us (100%)
    pallas_call x1, Pallas kernels, shards(): pl.pallas_call(functools.partial(kernel, doms, bands, nb, nx, ny, nz), ou...  98.2 us

profile of v3, /device:TPU:0, one launch (start us, length us, event | category | flops | bytes accessed | tf_op | source)
XLA Modules:
  0.0 100.1 jit_solution(6758488021465925519)
XLA Ops:
  0.0 98.2 %shard_map.28.held = f32[8,768,128]{2,1,0:T(8,128)S(1)} custom-call(f32[8,12,64,128]{3,2,1,0:T(8,128)} %orb.1, f32[768,128]{1,0:T(8,128)} %bitcast.2), custom_call_target="tpu_custom_call" | custom-call | tf_op jit(solution)/shard_map/pallas_call | solution.py:545
  98.3 1.7 %shard_map.29 = f32[8,768,128]{2,1,0:T(8,128)} custom-call(f32[8,768,128]{2,1,0:T(8,128)S(1)} %shard_map.28.held), custom_call_target="tpu_custom_call" | custom-call | tf_op jit(solution)/shard_map/pallas_call | solution.py:595
